TPU v7x, 32 devices: a whole 2x2x4 slice. The times are simulated.
32 devices in a mesh: visit: 8 (over y, x, core), sky: 4 (over z).
Axes of the slice: x: 2, y: 2, z: 4, core: 2. Of those that a mesh axis runs over, the one named last changes fastest.
Arguments:
- science: float32 [8, 16, 128, 128], P('visit', 'sky'), may hold values from -6 to 6
- coef_first: float32 [8, 16, 3, 49], P('visit', 'sky'), may hold values from -4 to 4
- coef_second: float32 [8, 16, 3, 49], P('visit', 'sky'), may hold values from -4 to 4
- weight: float32 [8, 16], P('visit', 'sky'), may hold values from 0.3 to 3
- slot_tile: int32 [8, 16], P('visit', 'sky'), may hold values from 0 to 3, as said below
- offsets: int32 [8, 16, 2], P('visit', 'sky'), may hold values from 0 to 128
- counts: int32 [8, 4], P('visit', 'sky'), may hold values from 3 to 4, as said below
- tile_place: int32 [4], replicated, may hold values from 0 to 3, as said below
Outputs:
- template: float32 [4, 256, 256], P('sky')
- difference: float32 [8, 16, 128, 128], P('visit', 'sky')
Inputs may be any that keep to these rules, and one draw needn't show every extreme that they name: `slot_tile`: among the usable slots of one device's list at most 2 name tiles of one owner; in every visit the tile of some owner gets exactly 2 usable slots from every device of the sky axis. A permutation: tile t is owned by the device of sky index tile_place[t]. The first counts[v, s] slots of a device's list are usable; in every visit some device has all 4 usable.
All inputs are finite; a program needn't handle non-finite values.
Results may differ from a plain program's by a relative error of at most 0.00011.
Values sent between devices are 32-bit elements; how exact they have to be, the bound alone decides.
No kernel may reach another device: no remote copies, remote signals or barrier semaphores. Data moves between devices by JAX's collectives and lax.ppermute only.
A program may use at most 64 MiB of HBM per device.

v0:
```python
import jax
import jax.numpy as jnp
from jax import lax
from jax.sharding import PartitionSpec as P

TILE = 256
TAPS = 21
PROFILES = 7
WIDTHS = (1.0, 1.0, 1.0, 2.5, 2.5, 2.5, 5.0)
POWERS = (0, 1, 2, 0, 1, 2, 0)
PRECISE = lax.Precision.HIGHEST


def profile_filters(side):
    reach = (TAPS - 1) // 2
    places = jnp.arange(side).astype(jnp.float32)
    spacing = places[None, :] - places[:, None]
    support = jnp.arange(TAPS).astype(jnp.float32) - reach
    stacked = []
    for number in range(PROFILES):
        sample = support ** POWERS[number] * jnp.exp(
            -support * support / (2.0 * WIDTHS[number] ** 2)
        )
        norming = jnp.sqrt(jnp.sum(sample * sample))
        values = spacing ** POWERS[number] * jnp.exp(
            -spacing * spacing / (2.0 * WIDTHS[number] ** 2)
        )
        stacked.append(jnp.where(jnp.abs(spacing) <= reach, values / norming, 0.0))
    return jnp.stack(stacked)


def positions(side):
    places = jnp.arange(side).astype(jnp.float32)
    return (2.0 * places - (side - 1)) / (side - 1)


def kernel_pass(block, coeffs, filters, spread):
    across_x = jnp.einsum("yw,ixw->iyx", block, filters, precision=PRECISE)
    layout = coeffs.reshape(3, PROFILES, PROFILES)
    plain = jnp.einsum("ij,jab->iab", layout[0], filters, precision=PRECISE)
    along = jnp.einsum("ij,jab->iab", layout[2], filters, precision=PRECISE) * spread[None, :, None]
    sideways = jnp.einsum("ij,jab->iab", layout[1], filters, precision=PRECISE)
    steady = jnp.einsum("iab,ibx->ax", plain + along, across_x, precision=PRECISE)
    varying = jnp.einsum("iab,ibx->ax", sideways, across_x, precision=PRECISE)
    return steady + varying * spread[None, :]


def body(science, coef_first, coef_second, weight, slot_tile, offsets, counts, tile_place):
    slots = science.shape[1]
    side = science.shape[2]
    owners_count = lax.axis_size("sky")
    capacity = max(2, (slots + owners_count - 1) // owners_count)
    buffer_slots = owners_count * capacity
    filters = profile_filters(side)
    spread = positions(side)
    listed = jnp.arange(slots)
    usable = listed < counts[0, 0]
    tile_ids = jnp.arange(tile_place.shape[0])
    owners = jnp.sum(
        jnp.where(slot_tile[0][:, None] == tile_ids[None, :], tile_place[None, :], 0), axis=1
    )
    convolved = lax.map(
        lambda operands: kernel_pass(operands[0], operands[1], filters, spread),
        (science[0], coef_first[0]),
    )
    sharing = (
        (owners[:, None] == owners[None, :]) & usable[None, :] & (listed[None, :] < listed[:, None])
    )
    earlier = jnp.sum(sharing.astype(jnp.int32), axis=1)
    target = jnp.where(usable, owners * capacity + earlier, -1)
    routing = (target[None, :] == jnp.arange(buffer_slots)[:, None]).astype(jnp.float32)
    packed = jnp.dot(routing, convolved.reshape(slots, side * side), precision=PRECISE).reshape(
        buffer_slots, side, side
    )
    sent_weight = jnp.dot(routing, weight[0], precision=PRECISE)
    sent_corner = jnp.dot(routing, offsets[0].astype(jnp.float32), precision=PRECISE)
    arrived, arrived_weight, arrived_corner = (
        lax.all_to_all(packed, "sky", split_axis=0, concat_axis=0, tiled=True),
        lax.all_to_all(sent_weight, "sky", split_axis=0, concat_axis=0, tiled=True),
        lax.all_to_all(sent_corner, "sky", split_axis=0, concat_axis=0, tiled=True),
    )
    corners = arrived_corner.astype(jnp.int32)

    def place_block(position, totals):
        weighted, coverage = totals
        corner_top = corners[position, 0]
        corner_left = corners[position, 1]
        block_weight = arrived_weight[position]
        region = lax.dynamic_slice(weighted, (corner_top, corner_left), (side, side))
        weighted = lax.dynamic_update_slice(
            weighted, region + block_weight * arrived[position], (corner_top, corner_left)
        )
        region = lax.dynamic_slice(coverage, (corner_top, corner_left), (side, side))
        coverage = lax.dynamic_update_slice(
            coverage, region + block_weight, (corner_top, corner_left)
        )
        return (weighted, coverage)

    empty = jnp.zeros((TILE, TILE), jnp.float32)
    weighted, coverage = lax.fori_loop(0, buffer_slots, place_block, (empty, empty))
    weighted, coverage = lax.psum((weighted, coverage), "visit")
    template = weighted / (coverage + 1.0)
    cut_back = jax.vmap(
        lambda corner: lax.dynamic_slice(template, (corner[0], corner[1]), (side, side))
    )(corners)
    returned = lax.all_to_all(cut_back, "sky", split_axis=0, concat_axis=0, tiled=True)
    cutouts = jnp.dot(
        routing.T, returned.reshape(buffer_slots, side * side), precision=PRECISE
    ).reshape(slots, side, side)
    matched = lax.map(
        lambda operands: kernel_pass(operands[0], operands[1], filters, spread),
        (cutouts, coef_second[0]),
    )
    difference = jnp.where(usable[:, None, None], science[0] - matched, 0.0)
    return (template[None], difference[None])


def solution(mesh):
    in_specs = (
        P("visit", "sky", None, None),
        P("visit", "sky", None, None),
        P("visit", "sky", None, None),
        P("visit", "sky"),
        P("visit", "sky"),
        P("visit", "sky", None),
        P("visit", "sky"),
        P(),
    )
    out_specs = (P("sky", None, None), P("visit", "sky", None, None))
    return jax.shard_map(body, mesh=mesh, in_specs=in_specs, out_specs=out_specs, check_vma=False)
```

profile of v0, /device:TPU:0, one launch (start us, length us, event | category | flops | bytes accessed | tf_op | source)
XLA Modules:
  0.0 270.1 jit_solution(13443177923790171623)
XLA Ops:
  9.8 6.3 %all-to-all-start.1 = ((f32[4,2,1]{1,2,0:T(1,128)}), f32[4,2,1]{1,2,0:T(1,128)S(1)}, u32[]{:S(2)}, u32[]{:S(2)}) async-start(f32[4,2,1]{1,2,0:T(1,128)} %copy.57), calls=%async_computation.1 | async-start | bytes 4096 | tf_op jit(solution)/shard_map/all_to_all | solution.py:79
  27.8 15.7 %while.42 = (s32[]{:T(128)}, f32[4,128,128]{2,1,0:T(8,128)S(1)}, f32[4,3,49]{2,1,0:T(4,128)S(1)}, f32[7,128,128]{2,0,1:T(8,128)S(1)}, f32[4,128,128]{2,1,0:T(8,128)S(1)}, /*index=5*/s32[]{:T(128)}) while((s32[]{:T(128)}, f32[4,128,128]{2,1,0:T(8,128)S(1)}, f32[4,3,49]{2,1,0:T(4,128)S(1)}, ...), condition=%wide.region_10.11_spmd.clone.clone, body=%wide.region_9.10_spmd.clone.clone.sunk | while | flops 557646336 | bytes 6362725 | solution.py:62
  45.0 5.1 %all-to-all-start = ((f32[4,2,2]{2,1,0:T(2,128)}), f32[4,2,2]{2,1,0:T(2,128)S(1)}, u32[]{:S(2)}, u32[]{:S(2)}) async-start(f32[4,2,2]{2,1,0:T(2,128)} %fusion.28), calls=%async_computation | async-start | bytes 8192 | tf_op jit(solution)/shard_map/all_to_all | solution.py:80
  51.0 4.7 %all-to-all-done = f32[4,2,2]{2,1,0:T(2,128)S(1)} async-done(((f32[4,2,2]{2,1,0:T(2,128)}), f32[4,2,2]{2,1,0:T(2,128)S(1)}, u32[]{:S(2)}, u32[]{:S(2)}) %all-to-all-start) | async-done | bytes 96 | tf_op jit(solution)/shard_map/all_to_all | solution.py:80
  55.6 3.5 %all-to-all-start.2 = ((f32[8,128,128]{2,1,0:T(8,128)}), f32[8,128,128]{2,1,0:T(8,128)S(1)}, u32[]{:S(2)}, u32[]{:S(2)}) async-start(f32[8,128,128]{2,1,0:T(8,128)} %copy.59), calls=%async_computation.2 | async-start | bytes 1048576 | tf_op jit(solution)/shard_map/all_to_all | solution.py:78
  60.7 11.1 %all-to-all-done.2 = f32[8,128,128]{2,1,0:T(8,128)S(1)} async-done(((f32[8,128,128]{2,1,0:T(8,128)}), f32[8,128,128]{2,1,0:T(8,128)S(1)}, u32[]{:S(2)}, u32[]{:S(2)}) %all-to-all-start.2) | async-done | bytes 524320 | tf_op jit(solution)/shard_map/all_to_all | solution.py:78
  71.9 77.3 %while.40 = (s32[]{:T(128)}, f32[256,256]{1,0:T(8,128)S(1)}, f32[256,256]{1,0:T(8,128)S(1)}, s32[8,2]{0,1:T(2,128)S(1)}, f32[8]{0:T(128)S(1)}, /*index=5*/f32[8,...) while((s32[]{:T(128)}, f32[256,256]{1,0:T(8,128)S(1)}, f32[256,256]{1,0:T(8,128)S(1)}, ...), condition=%wide.region_12.13_spmd, body=%wide.region_11.12_spmd.sunk | while | flops 49160 | bytes 591569 | solution.py:100
  78.0 2.0 dynamic_update_slice.32
  79.9 2.0 dynamic_update_slice.31
  88.0 1.9 dynamic_update_slice.32
  89.9 1.9 dynamic_update_slice.31
  97.9 2.0 dynamic_update_slice.32
  99.9 2.0 dynamic_update_slice.31
  107.9 1.7 dynamic_update_slice.32
  117.3 1.9 dynamic_update_slice.32
  119.2 1.9 dynamic_update_slice.31
  127.1 1.7 dynamic_update_slice.32
  128.8 1.7 dynamic_update_slice.31
  136.5 1.7 dynamic_update_slice.32
  150.1 54.8 %all-reduce.3.cloned.1.call-done = (f32[256,256]{1,0:T(8,128)}, f32[256,256]{1,0:T(8,128)}) async-done(((f32[256,256]{1,0:T(8,128)}, f32[256,256]{1,0:T(8,128)}), (f32[256,256]{1,0:T(8,128)}, f32[256,256]{1,0:T(8,128)})) %all-reduce.3.cloned.1.call-update) | async-done | bytes 524304 | tf_op jit(solution)/shard_map/psum | solution.py:101
  205.9 20.8 %while.41 = (s32[]{:T(128)}, f32[256,256]{1,0:T(8,128)S(1)}, s32[8,2]{0,1:T(2,128)S(1)}, f32[8,128,128]{2,1,0:T(8,128)}, s32[]{:T(128)}) while((s32[]{:T(128)}, f32[256,256]{1,0:T(8,128)S(1)}, s32[8,2]{0,1:T(2,128)S(1)}, f32[8,128,128]{2,1,0:T(8,128)}, s32[]{:T(128)}) %tuple.118), condition=%wide.while_cond, body=%wide.while_body.sunk | while | flops 2 | bytes 132705 | solution.py:104
  206.6 2.0 bitcast_dynamic-update-slice_fusion.2
  209.2 2.0 bitcast_dynamic-update-slice_fusion.2
  211.8 2.0 bitcast_dynamic-update-slice_fusion.2
  214.4 2.0 bitcast_dynamic-update-slice_fusion.2
  217.0 2.0 bitcast_dynamic-update-slice_fusion.2
  219.5 2.0 bitcast_dynamic-update-slice_fusion.2
  222.2 2.0 bitcast_dynamic-update-slice_fusion.2
  224.8 2.0 bitcast_dynamic-update-slice_fusion.2
  227.5 4.6 %all-to-all-start.3 = ((f32[8,128,128]{2,1,0:T(8,128)}), f32[8,128,128]{2,1,0:T(8,128)S(1)}, u32[]{:S(2)}, u32[]{:S(2)}) async-start(f32[8,128,128]{2,1,0:T(8,128)} %get-tuple-element.193), calls=%async_computation.3 | async-start | bytes 1048576 | tf_op jit(solution)/shard_map/all_to_all | solution.py:106
  232.0 13.8 %all-to-all-done.3 = f32[8,128,128]{2,1,0:T(8,128)S(1)} async-done(((f32[8,128,128]{2,1,0:T(8,128)}), f32[8,128,128]{2,1,0:T(8,128)S(1)}, u32[]{:S(2)}, u32[]{:S(2)}) %all-to-all-start.3) | async-done | bytes 524320 | tf_op jit(solution)/shard_map/all_to_all | solution.py:106
  246.5 16.0 %while.43 = (s32[]{:T(128)}, f32[4,128,128]{2,1,0:T(8,128)S(1)}, f32[4,3,49]{2,1,0:T(4,128)S(1)}, f32[7,128,128]{2,0,1:T(8,128)S(1)}, f32[4,128,128]{2,0,1:T(4,128)S(1)}, /*index=5*/s32[]{:T(128)}) while((s32[]{:T(128)}, f32[4,128,128]{2,1,0:T(8,128)S(1)}, f32[4,3,49]{2,1,0:T(4,128)S(1)}, ...), condition=%wide.region_16.17_spmd.clone.clone, body=%wide.region_15.16_spmd.clone.clone.sunk | while | flops 557646336 | bytes 6428261 | solution.py:110
  (207 shorter events, 75.5 us)
Async XLA Ops:
  7.2 1.8 copy-start
  7.8 0.7 copy-start.8
  7.9 0.7 copy-start.9
  9.8 35.1 %all-to-all-start.1 = ((f32[4,2,1]{1,2,0:T(1,128)}), f32[4,2,1]{1,2,0:T(1,128)S(1)}, u32[]{:S(2)}, u32[]{:S(2)}) async-start(f32[4,2,1]{1,2,0:T(1,128)} %copy.57), calls=%async_computation.1 | async-start | bytes 4096 | tf_op jit(solution)/shard_map/all_to_all | solution.py:79
  22.7 2.7 %copy-start.5 = (f32[1,4,3,49]{3,1,2,0:T(4,128)S(1)}, f32[1,4,3,49]{3,1,2,0:T(4,128)}, u32[]{:S(2)}) copy-start(f32[1,4,3,49]{3,1,2,0:T(4,128)} %param.15) | copy-start | bytes 7060
  26.8 1.0 copy-start.4
  43.5 0.7 copy-start.7
  45.0 10.7 %all-to-all-start = ((f32[4,2,2]{2,1,0:T(2,128)}), f32[4,2,2]{2,1,0:T(2,128)S(1)}, u32[]{:S(2)}, u32[]{:S(2)}) async-start(f32[4,2,2]{2,1,0:T(2,128)} %fusion.28), calls=%async_computation | async-start | bytes 8192 | tf_op jit(solution)/shard_map/all_to_all | solution.py:80
  55.6 16.2 %all-to-all-start.2 = ((f32[8,128,128]{2,1,0:T(8,128)}), f32[8,128,128]{2,1,0:T(8,128)S(1)}, u32[]{:S(2)}, u32[]{:S(2)}) async-start(f32[8,128,128]{2,1,0:T(8,128)} %copy.59), calls=%async_computation.2 | async-start | bytes 1048576 | tf_op jit(solution)/shard_map/all_to_all | solution.py:78
  59.1 145.8 %all-reduce.3.cloned.1.call-start = ((), (), s32[]{:S(2)}) async-start(), calls=%async_computation.4 | async-start | bytes 1048576 | tf_op jit(solution)/shard_map/psum | solution.py:101
  149.2 0.7 copy-start.1
  149.3 0.8 copy-start.2
  226.8 0.7 copy-start.3
  226.8 5.3 %copy-start.6 = (f32[1,4,3,49]{3,1,2,0:T(4,128)S(1)}, f32[1,4,3,49]{3,1,2,0:T(4,128)}, u32[]{:S(2)}) copy-start(f32[1,4,3,49]{3,1,2,0:T(4,128)} %param.16) | copy-start | bytes 7060
  227.5 18.3 %all-to-all-start.3 = ((f32[8,128,128]{2,1,0:T(8,128)}), f32[8,128,128]{2,1,0:T(8,128)S(1)}, u32[]{:S(2)}, u32[]{:S(2)}) async-start(f32[8,128,128]{2,1,0:T(8,128)} %get-tuple-element.193), calls=%async_computation.3 | async-start | bytes 1048576 | tf_op jit(solution)/shard_map/all_to_all | solution.py:106
Sparse Core Ops, SparseCore 0:
  150.2 54.6 all-reduce.2
where the time goes:
time: 271 us; the launch traced here: 270 us
  waiting for transfers between devices  84.3 us (31%)
  local copies, waits for them, and re-layouts  68.5 us (25%)
  loops' own time  33 us (12%)
  matrix products  30.9 us (11%)
  between operations  19.6 us (7%)
  starting transfers between devices  19.5 us (7%)
  other arithmetic  14.3 us (5%)
    psum x1, waiting for transfers between devices, body(): weighted, coverage = lax.psum((weighted, coverage), 'visit')  54.8 us
    another operation x1, loops' own time, body(): lax.fori_loop(0, buffer_slots, place_block, (empty, empty))  32.4 us
    gather x24, local copies, waits for them, and re-layouts  20.8 us
    dynamic_update_slice x8, local copies, waits for them, and re-layouts, place_block(): lax.dynamic_update_slice(coverage, region + block_weight, (corner_top, co...  14.4 us
    dynamic_update_slice x8, local copies, waits for them, and re-layouts, place_block(): lax.dynamic_update_slice(weighted, region + block_weight * arrived[positi...  14.4 us
    all_to_all x1, waiting for transfers between devices, body(): lax.all_to_all(cut_back, 'sky', split_axis=0, concat_axis=0, tiled=True)  13.8 us
    all_to_all x1, waiting for transfers between devices, body(): lax.all_to_all(packed, 'sky', split_axis=0, concat_axis=0, tiled=True)  11.1 us
    all_to_all x1, starting transfers between devices, body(): lax.all_to_all(sent_weight, 'sky', split_axis=0, concat_axis=0, tiled=True)  6.35 us
  transfers between devices with their start and end apart: 5, of which 4 were waited for; matrix products, arithmetic and copies ran while one was open for 9% of the time, Pallas kernels for 0%

commit v1 on v0

--- a/solution.py
+++ b/solution.py
@@ -9,6 +9,22 @@
 WIDTHS = (1.0, 1.0, 1.0, 2.5, 2.5, 2.5, 5.0)
 POWERS = (0, 1, 2, 0, 1, 2, 0)
 PRECISE = lax.Precision.HIGHEST
+
+
+def exchange_in_pairs(x, axis, split, join):
+    ways, here = (lax.axis_size(axis), lax.axis_index(axis))
+    width = x.shape[split] // ways
+    lengths = list(x.shape)
+    lengths[split] = width
+    height = lengths[join]
+    lengths[join] = height * ways
+    full = jnp.zeros(lengths, x.dtype)
+    for mask in range(ways):
+        part = lax.dynamic_slice_in_dim(x, (here ^ mask) * width, width, axis=split)
+        if mask:
+            part = lax.ppermute(part, axis, [(d, d ^ mask) for d in range(ways)])
+        full = lax.dynamic_update_slice_in_dim(full, part, (here ^ mask) * height, axis=join)
+    return full
 
 
 def profile_filters(side):
@@ -75,7 +91,7 @@
     sent_weight = jnp.dot(routing, weight[0], precision=PRECISE)
     sent_corner = jnp.dot(routing, offsets[0].astype(jnp.float32), precision=PRECISE)
     arrived, arrived_weight, arrived_corner = (
-        lax.all_to_all(packed, "sky", split_axis=0, concat_axis=0, tiled=True),
+        exchange_in_pairs(packed, "sky", 0, 0),
         lax.all_to_all(sent_weight, "sky", split_axis=0, concat_axis=0, tiled=True),
         lax.all_to_all(sent_corner, "sky", split_axis=0, concat_axis=0, tiled=True),
     )

time: 271 us -> 263 us (0.970)
  waiting for transfers between devices: 84.3 us -> 77.2 us
    all_to_all x1 -> x0, waiting for transfers between devices: 11.1 us -> none  [body(): lax.all_to_all(packed, 'sky', split_axis=0, concat_axis=0, tiled=True)]
    ppermute x0 -> x3, starting transfers between devices: none -> 5.71 us  [exchange_in_pairs(): part = lax.ppermute(part, axis, [(d, d ^ mask) for d in range(ways)])]
    all_to_all x1, waiting for transfers between devices: 0.01 us -> 4.29 us  [body(): lax.all_to_all(sent_weight, 'sky', split_axis=0, concat_axis=0, tiled=True)]
    all_to_all x1 -> x0, starting transfers between devices: 3.47 us -> none  [body(): lax.all_to_all(packed, 'sky', split_axis=0, concat_axis=0, tiled=True)]
  transfers between devices with their start and end apart: 5 -> 7, of which waited for: 4 -> 4; matrix products, arithmetic and copies ran while one was open for 9% -> 1% of each run, Pallas kernels for 0% -> 0%
where the time goes in v1:
time: 263 us; the launch traced here: 262 us
  waiting for transfers between devices  77.2 us (29%)
  local copies, waits for them, and re-layouts  68.6 us (26%)
  loops' own time  32 us (12%)
  matrix products  30.9 us (12%)
  between operations  19.7 us (7%)
  starting transfers between devices  19.1 us (7%)
  other arithmetic  14.3 us (5%)
    psum x1, waiting for transfers between devices, body(): weighted, coverage = lax.psum((weighted, coverage), 'visit')  54.8 us
    another operation x1, loops' own time, body(): lax.fori_loop(0, buffer_slots, place_block, (empty, empty))  31.4 us
    gather x24, local copies, waits for them, and re-layouts  20.8 us
    dynamic_update_slice x8, local copies, waits for them, and re-layouts, place_block(): lax.dynamic_update_slice(weighted, region + block_weight * arrived[positi...  14.4 us
    dynamic_update_slice x8, local copies, waits for them, and re-layouts, place_block(): lax.dynamic_update_slice(coverage, region + block_weight, (corner_top, co...  14.4 us
    all_to_all x1, waiting for transfers between devices, body(): lax.all_to_all(cut_back, 'sky', split_axis=0, concat_axis=0, tiled=True)  13.7 us
    add x8, other arithmetic, place_block(): region + block_weight * arrived[position]  6.03 us
    ppermute x3, starting transfers between devices, exchange_in_pairs(): part = lax.ppermute(part, axis, [(d, d ^ mask) for d in range(ways)])  5.71 us
  transfers between devices with their start and end apart: 7, of which 4 were waited for; matrix products, arithmetic and copies ran while one was open for 1% of the time, Pallas kernels for 0%

profile of v1, /device:TPU:0, one launch (start us, length us, event | category | flops | bytes accessed | tf_op | source)
XLA Modules:
  0.0 261.7 jit_solution(1871796020282940721)
XLA Ops:
  18.8 15.7 %while.42 = (s32[]{:T(128)}, f32[4,128,128]{2,1,0:T(8,128)S(1)}, f32[4,3,49]{2,1,0:T(4,128)S(1)}, f32[7,128,128]{2,0,1:T(8,128)S(1)}, f32[4,128,128]{2,1,0:T(8,128)S(1)}, /*index=5*/s32[]{:T(128)}) while((s32[]{:T(128)}, f32[4,128,128]{2,1,0:T(8,128)S(1)}, f32[4,3,49]{2,1,0:T(4,128)S(1)}, ...), condition=%wide.region_10.11_spmd.clone.clone, body=%wide.region_9.10_spmd.clone.clone.sunk | while | flops 557646336 | bytes 6362725 | solution.py:78
  37.1 3.1 %collective-permute-start = (f32[2,128,128]{2,0,1:T(2,128)S(1)}, f32[2,128,128]{2,0,1:T(2,128)S(1)}, u32[]{:S(2)}, u32[]{:S(2)}) collective-permute-start(f32[2,128,128]{2,0,1:T(2,128)S(1)} %get-tuple-element.331), channel_id=1, source_target_pairs={{0,1},{1,0},{2,3},{3,2},{4,5},{5,4},{6,7},{7,6},{8,9},{9,8},{10,11... | collective-permute-start | bytes 393224 | tf_op jit(solution)/shard_map/ppermute | solution.py:25
  40.2 2.6 collective-permute-start.1
  43.7 5.1 %all-to-all-start.1 = ((f32[4,2,1]{1,2,0:T(1,128)}), f32[4,2,1]{1,2,0:T(1,128)S(1)}, u32[]{:S(2)}, u32[]{:S(2)}) async-start(f32[4,2,1]{1,2,0:T(1,128)} %copy.69), calls=%async_computation.1 | async-start | bytes 4096 | tf_op jit(solution)/shard_map/all_to_all | solution.py:95
  50.3 4.3 %all-to-all-done.1 = f32[4,2,1]{1,2,0:T(1,128)S(1)} async-done(((f32[4,2,1]{1,2,0:T(1,128)}), f32[4,2,1]{1,2,0:T(1,128)S(1)}, u32[]{:S(2)}, u32[]{:S(2)}) %all-to-all-start.1) | async-done | bytes 64 | tf_op jit(solution)/shard_map/all_to_all | solution.py:95
  54.6 3.7 %all-to-all-start = ((f32[4,2,2]{2,1,0:T(2,128)}), f32[4,2,2]{2,1,0:T(2,128)S(1)}, u32[]{:S(2)}, u32[]{:S(2)}) async-start(f32[4,2,2]{2,1,0:T(2,128)} %fusion.28), calls=%async_computation | async-start | bytes 8192 | tf_op jit(solution)/shard_map/all_to_all | solution.py:96
  59.6 4.3 %all-to-all-done = f32[4,2,2]{2,1,0:T(2,128)S(1)} async-done(((f32[4,2,2]{2,1,0:T(2,128)}), f32[4,2,2]{2,1,0:T(2,128)S(1)}, u32[]{:S(2)}, u32[]{:S(2)}) %all-to-all-start) | async-done | bytes 96 | tf_op jit(solution)/shard_map/all_to_all | solution.py:96
  64.3 75.6 %while.40 = (s32[]{:T(128)}, f32[256,256]{1,0:T(8,128)S(1)}, f32[256,256]{1,0:T(8,128)S(1)}, s32[8,2]{0,1:T(2,128)S(1)}, f32[8]{0:T(128)S(1)}, /*index=5*/f32[8,...) while((s32[]{:T(128)}, f32[256,256]{1,0:T(8,128)S(1)}, f32[256,256]{1,0:T(8,128)S(1)}, ...), condition=%wide.region_12.13_spmd, body=%wide.region_11.12_spmd.sunk | while | flops 49160 | bytes 591569 | solution.py:116
  70.2 2.0 dynamic_update_slice.52
  72.1 2.0 dynamic_update_slice.51
  80.0 1.9 dynamic_update_slice.52
  81.9 1.9 dynamic_update_slice.51
  89.7 2.0 dynamic_update_slice.52
  91.7 2.0 dynamic_update_slice.51
  99.5 1.7 dynamic_update_slice.52
  101.2 1.7 dynamic_update_slice.51
  108.7 1.9 dynamic_update_slice.52
  110.6 1.9 dynamic_update_slice.51
  118.3 1.7 dynamic_update_slice.52
  140.8 54.8 %all-reduce.3.cloned.1.call-done = (f32[256,256]{1,0:T(8,128)}, f32[256,256]{1,0:T(8,128)}) async-done(((f32[256,256]{1,0:T(8,128)}, f32[256,256]{1,0:T(8,128)}), (f32[256,256]{1,0:T(8,128)}, f32[256,256]{1,0:T(8,128)})) %all-reduce.3.cloned.1.call-update) | async-done | bytes 524304 | tf_op jit(solution)/shard_map/psum | solution.py:117
  197.5 20.8 %while.41 = (s32[]{:T(128)}, f32[256,256]{1,0:T(8,128)S(1)}, s32[8,2]{0,1:T(2,128)S(1)}, f32[8,128,128]{2,1,0:T(8,128)}, s32[]{:T(128)}) while((s32[]{:T(128)}, f32[256,256]{1,0:T(8,128)S(1)}, s32[8,2]{0,1:T(2,128)S(1)}, f32[8,128,128]{2,1,0:T(8,128)}, s32[]{:T(128)}) %tuple.119), condition=%wide.while_cond, body=%wide.while_body.sunk | while | flops 2 | bytes 132705 | solution.py:120
  198.1 2.0 bitcast_dynamic-update-slice_fusion.2
  200.7 2.0 bitcast_dynamic-update-slice_fusion.2
  203.3 2.0 bitcast_dynamic-update-slice_fusion.2
  205.9 2.0 bitcast_dynamic-update-slice_fusion.2
  208.5 2.0 bitcast_dynamic-update-slice_fusion.2
  211.1 2.0 bitcast_dynamic-update-slice_fusion.2
  213.7 2.0 bitcast_dynamic-update-slice_fusion.2
  216.3 2.0 bitcast_dynamic-update-slice_fusion.2
  219.0 4.6 %all-to-all-start.2 = ((f32[8,128,128]{2,1,0:T(8,128)}), f32[8,128,128]{2,1,0:T(8,128)S(1)}, u32[]{:S(2)}, u32[]{:S(2)}) async-start(f32[8,128,128]{2,1,0:T(8,128)} %get-tuple-element.193), calls=%async_computation.2 | async-start | bytes 1048576 | tf_op jit(solution)/shard_map/all_to_all | solution.py:122
  223.6 13.7 %all-to-all-done.2 = f32[8,128,128]{2,1,0:T(8,128)S(1)} async-done(((f32[8,128,128]{2,1,0:T(8,128)}), f32[8,128,128]{2,1,0:T(8,128)S(1)}, u32[]{:S(2)}, u32[]{:S(2)}) %all-to-all-start.2) | async-done | bytes 524320 | tf_op jit(solution)/shard_map/all_to_all | solution.py:122
  238.0 16.0 %while.43 = (s32[]{:T(128)}, f32[4,128,128]{2,1,0:T(8,128)S(1)}, f32[4,3,49]{2,1,0:T(4,128)S(1)}, f32[7,128,128]{2,0,1:T(8,128)S(1)}, f32[4,128,128]{2,0,1:T(4,128)S(1)}, /*index=5*/s32[]{:T(128)}) while((s32[]{:T(128)}, f32[4,128,128]{2,1,0:T(8,128)S(1)}, f32[4,3,49]{2,1,0:T(4,128)S(1)}, ...), condition=%wide.region_16.17_spmd.clone.clone, body=%wide.region_15.16_spmd.clone.clone.sunk | while | flops 557646336 | bytes 6428261 | solution.py:126
  (216 shorter events, 77.3 us)
Async XLA Ops:
  7.2 35.7 %copy-start = (f32[1,4]{1,0:T(1,128)S(1)}, f32[1,4]{1,0:T(1,128)}, u32[]{:S(2)}) copy-start(f32[1,4]{1,0:T(1,128)} %param.17) | copy-start | bytes 52
  12.3 4.1 %copy-start.5 = (f32[1,4,3,49]{3,1,2,0:T(4,128)S(1)}, f32[1,4,3,49]{3,1,2,0:T(4,128)}, u32[]{:S(2)}) copy-start(f32[1,4,3,49]{3,1,2,0:T(4,128)} %param.15) | copy-start | bytes 7060
  17.8 1.0 copy-start.4
  35.2 0.7 copy-start.8
  35.2 0.7 copy-start.9
  37.1 27.1 %collective-permute-start = (f32[2,128,128]{2,0,1:T(2,128)S(1)}, f32[2,128,128]{2,0,1:T(2,128)S(1)}, u32[]{:S(2)}, u32[]{:S(2)}) collective-permute-start(f32[2,128,128]{2,0,1:T(2,128)S(1)} %get-tuple-element.331), channel_id=1, source_target_pairs={{0,1},{1,0},{2,3},{3,2},{4,5},{5,4},{6,7},{7,6},{8,9},{9,8},{10,11... | collective-permute-start | bytes 393224 | tf_op jit(solution)/shard_map/ppermute | solution.py:25
  40.2 24.0 %collective-permute-start.1 = (f32[2,128,128]{2,0,1:T(2,128)S(1)}, f32[2,128,128]{2,0,1:T(2,128)S(1)}, u32[]{:S(2)}, u32[]{:S(2)}) collective-permute-start(f32[2,128,128]{2,0,1:T(2,128)S(1)} %get-tuple-element.330), channel_id=1, source_target_pairs={{0,2},{1,3},{2,0},{3,1},{4,6},{5,7},{6,4},{7,5},{8,10},{9,11},{10,... | collective-permute-start | bytes 393224 | tf_op jit(solution)/shard_map/ppermute | solution.py:25
  42.8 21.5 %collective-permute-start.2 = (f32[2,128,128]{2,0,1:T(2,128)S(1)}, f32[2,128,128]{2,0,1:T(2,128)S(1)}, u32[]{:S(2)}, u32[]{:S(2)}) collective-permute-start(f32[2,128,128]{2,0,1:T(2,128)S(1)} %get-tuple-element.329), channel_id=1, source_target_pairs={{0,3},{1,2},{2,1},{3,0},{4,7},{5,6},{6,5},{7,4},{8,11},{9,10},{10,... | collective-permute-start | bytes 393224 | tf_op jit(solution)/shard_map/ppermute | solution.py:25
  43.7 10.8 %all-to-all-start.1 = ((f32[4,2,1]{1,2,0:T(1,128)}), f32[4,2,1]{1,2,0:T(1,128)S(1)}, u32[]{:S(2)}, u32[]{:S(2)}) async-start(f32[4,2,1]{1,2,0:T(1,128)} %copy.69), calls=%async_computation.1 | async-start | bytes 4096 | tf_op jit(solution)/shard_map/all_to_all | solution.py:95
  48.9 0.7 copy-start.7
  54.6 9.3 %all-to-all-start = ((f32[4,2,2]{2,1,0:T(2,128)}), f32[4,2,2]{2,1,0:T(2,128)S(1)}, u32[]{:S(2)}, u32[]{:S(2)}) async-start(f32[4,2,2]{2,1,0:T(2,128)} %fusion.28), calls=%async_computation | async-start | bytes 8192 | tf_op jit(solution)/shard_map/all_to_all | solution.py:96
  58.3 137.3 %all-reduce.3.cloned.1.call-start = ((), (), s32[]{:S(2)}) async-start(), calls=%async_computation.3 | async-start | bytes 1048576 | tf_op jit(solution)/shard_map/psum | solution.py:117
  140.0 0.7 copy-start.1
  140.0 0.8 copy-start.2
  218.3 0.7 copy-start.3
  218.3 5.3 %copy-start.6 = (f32[1,4,3,49]{3,1,2,0:T(4,128)S(1)}, f32[1,4,3,49]{3,1,2,0:T(4,128)}, u32[]{:S(2)}) copy-start(f32[1,4,3,49]{3,1,2,0:T(4,128)} %param.16) | copy-start | bytes 7060
  219.0 18.3 %all-to-all-start.2 = ((f32[8,128,128]{2,1,0:T(8,128)}), f32[8,128,128]{2,1,0:T(8,128)S(1)}, u32[]{:S(2)}, u32[]{:S(2)}) async-start(f32[8,128,128]{2,1,0:T(8,128)} %get-tuple-element.193), calls=%async_computation.2 | async-start | bytes 1048576 | tf_op jit(solution)/shard_map/all_to_all | solution.py:122
Sparse Core Ops, SparseCore 0:
  140.9 54.6 all-reduce.2
